TPU v7x, 32 devices: a whole 2x2x4 slice. The times are simulated.
32 devices in a mesh: groups: 2 (over y), zone: 4 (over x, core), tile: 4 (over z).
Axes of the slice: x: 2, y: 2, z: 4, core: 2. Of those that a mesh axis runs over, the one named last changes fastest.
Arguments:
- backscatter: bfloat16 [8, 2, 256, 512], P(('groups', 'zone'), None, 'tile'), parts along dimension 0, may hold values from -6 to 6
- row_bank: bfloat16 [16, 128, 128], replicated, may hold values from -0.3125 to 0.3125
- row_index: int32 [8, 4, 3], P(('groups', 'zone')), parts along dimension 0, may hold values from 0 to 3
- row_pick: int32 [8, 4, 3], P(('groups', 'zone')), parts along dimension 0, may hold values from 0 to 15
- row_mask: int32 [8, 4, 3], P(('groups', 'zone')), parts along dimension 0, may hold values 0 or 1
- column_bank: bfloat16 [16, 128, 128], replicated, may hold values from -0.3125 to 0.3125
- column_index: int32 [8, 2, 3], P(('groups', 'zone')), parts along dimension 0, may hold values from 0 to 1
- column_pick: int32 [8, 2, 3], P(('groups', 'zone')), parts along dimension 0, may hold values from 0 to 15
- column_mask: int32 [8, 2, 3], P(('groups', 'zone')), parts along dimension 0, may hold values 0 or 1
Outputs:
- geocoded: bfloat16 [8, 2, 256, 512], P(('groups', 'zone'), None, None, 'tile'), parts along dimension 0
There are 2 independent parts, one for each index of `groups`. A program takes and returns all parts, laid end to end along the dimension named above; an argument that names none is the same for every part. Nothing has to cross between parts.
All inputs are finite; a program needn't handle non-finite values. No bound on the sum of `row_mask` or of `column_mask` on one device may be relied on, other than what follows from the above.
Results may differ from a plain program's by a relative error of at most 0.0049.
Values may be sent and summed in bfloat16 or wider, within the bound.
No kernel may reach another device: no remote copies, remote signals or barrier semaphores. Data moves between devices by JAX's collectives and lax.ppermute only.
A program may use at most 64 MiB of HBM per device.

v0:
```python
import jax
import jax.numpy as jnp
from jax import lax
from jax.sharding import PartitionSpec as P

BLOCK = 128
EDGE = 64


def passed_along(block, axis, distance):
    devices = range(lax.axis_size(axis))
    route = [(i - distance, i) for i in devices if i - distance in devices]
    return lax.ppermute(block, axis, route)


def swap_panels(top_panel, bottom_panel):
    from_below = passed_along(top_panel, "zone", -1)
    from_above = passed_along(bottom_panel, "zone", 1)
    zone_index = lax.axis_index("zone")
    last_zone = lax.axis_size("zone") - 1
    feather = ((jnp.arange(EDGE, dtype=jnp.float32) + 0.5) / EDGE)[:, None]
    lower_blend = (
        (1.0 - feather) * bottom_panel.astype(jnp.float32)
        + feather * from_below.astype(jnp.float32)
    ).astype(jnp.bfloat16)
    upper_blend = (
        (1.0 - feather) * from_above.astype(jnp.float32) + feather * top_panel.astype(jnp.float32)
    ).astype(jnp.bfloat16)
    new_bottom = jnp.where(zone_index < last_zone, lower_blend, bottom_panel)
    new_top = jnp.where(zone_index > 0, upper_blend, top_panel)
    return (new_top, new_bottom)


def on_device(
    backscatter,
    row_bank,
    row_index,
    row_pick,
    row_mask,
    column_bank,
    column_index,
    column_pick,
    column_mask,
):
    image = backscatter[0]
    channels, lin_dev, samples = image.shape
    column_blocks = samples // BLOCK
    blocks = image.reshape(channels, lin_dev, column_blocks, BLOCK)
    gathered = blocks[:, :, row_index[0], :]
    row_weights = row_bank[row_pick[0]] * row_mask[0].astype(jnp.bfloat16)[:, :, None, None]
    along_samples = jnp.einsum(
        "clqbi,qbij->clqj", gathered, row_weights, preferred_element_type=jnp.float32
    )
    along_samples = along_samples.astype(jnp.bfloat16).reshape(channels, lin_dev, samples)
    line_blocks = column_index.shape[1]
    rows = line_blocks * BLOCK
    column_weights = (
        column_bank[column_pick[0]] * column_mask[0].astype(jnp.bfloat16)[:, :, None, None]
    )
    band_table = column_index[0]
    every_id = jnp.arange(line_blocks, dtype=jnp.int32)
    moved = lax.all_to_all(along_samples, "tile", split_axis=2, concat_axis=1, tiled=True)
    count = moved.shape[0]
    line_tiles = moved.reshape(count, line_blocks, BLOCK, BLOCK)
    picked = line_tiles[:, band_table[every_id]]
    result = jnp.einsum(
        "crbik,rboi->crok", picked, column_weights[every_id], preferred_element_type=jnp.float32
    )
    result = result.astype(jnp.bfloat16).reshape(count, every_id.shape[0] * BLOCK, BLOCK)
    new_top, new_bottom = swap_panels(result[:, :EDGE], result[:, rows - EDGE :])
    gridded = jnp.concatenate([new_top, result[:, EDGE : rows - EDGE], new_bottom], axis=1)
    return gridded[None]


def solution(mesh):
    in_specs = (
        P(("groups", "zone"), None, "tile", None),
        P(),
        P(("groups", "zone"), None, None),
        P(("groups", "zone"), None, None),
        P(("groups", "zone"), None, None),
        P(),
        P(("groups", "zone"), None, None),
        P(("groups", "zone"), None, None),
        P(("groups", "zone"), None, None),
    )
    out_specs = P(("groups", "zone"), None, None, "tile")
    return jax.shard_map(
        on_device, mesh=mesh, in_specs=in_specs, out_specs=out_specs, check_vma=False
    )
```

profile of v0, /device:TPU:1, one launch (start us, length us, event | category | flops | bytes accessed | tf_op | source)
XLA Modules:
  0.0 29.0 jit_solution(11059921443978826120)
XLA Ops:
  0.0 0.0 copy-start
  0.0 1.0 %reshape_squeeze.3 = bf16[2,64,4,128]{3,2,1,0:T(4,128)(2,1)S(1)} reshape(bf16[1,2,64,512]{3,2,1,0:T(8,128)(2,1)} %param.9) | data formatting | bytes 262144 | tf_op jit(solution)/shard_map/reshape;squeeze | solution.py:48
  1.0 0.0 copy-start.2
  1.0 0.6 %copy-done.2 = s32[1,4,3]{1,0,2:T(1,128)S(1)} copy-done((s32[1,4,3]{1,0,2:T(1,128)S(1)}, s32[1,4,3]{1,0,2:T(1,128)}, u32[]{:S(2)}) %copy-start.2) | copy-done | bytes 72
  1.7 0.1 copy.41
  1.8 0.1 reshape.158
  1.9 0.0 copy-start.3
  1.9 0.7 %copy-done.3 = s32[1,4,3]{1,0,2:T(1,128)S(1)} copy-done((s32[1,4,3]{1,0,2:T(1,128)S(1)}, s32[1,4,3]{1,0,2:T(1,128)}, u32[]{:S(2)}) %copy-start.3) | copy-done | bytes 72
  2.6 0.1 copy.39
  2.7 0.1 reshape.150
  2.7 0.0 copy-start.4
  2.8 0.7 %copy-done.4 = s32[1,4,3]{1,0,2:T(1,128)S(1)} copy-done((s32[1,4,3]{1,0,2:T(1,128)S(1)}, s32[1,4,3]{1,0,2:T(1,128)}, u32[]{:S(2)}) %copy-start.4) | copy-done | bytes 72
  3.4 0.1 copy.40
  3.5 0.6 %gather_fusion.3 = bf16[12,2,64,128]{3,2,1,0:T(8,128)(2,1)S(1)} fusion(bf16[2,64,4,128]{3,1,2,0:T(8,128)(2,1)S(1)} %copy.42, s32[1024]{0:T(1024)S(1)} %pad_clamp_fusion.1), kind=kCustom, calls=%fused_computation.3 | custom fusion | bytes 786480 | tf_op jit(solution)/shard_map/gather | solution.py:49
  4.2 0.0 copy-done
  4.2 0.6 %gather_fusion.2 = bf16[12,128,128]{2,1,0:T(8,128)(2,1)S(1)} fusion(bf16[16,128,128]{2,1,0:T(8,128)(2,1)S(1)} %copy-done, s32[1024]{0:T(1024)S(1)} %pad_clamp_fusion.2), kind=kCustom, calls=%fused_computation.2 | custom fusion | bytes 786480 | tf_op jit(solution)/shard_map/gather | solution.py:50
  4.8 0.3 %fusion.2 = bf16[2,64,4,128]{3,1,0,2:T(8,128)(2,1)S(1)} fusion(bf16[2,64,4,3,128]{4,1,0,3,2:T(8,128)(2,1)S(1)} %bitcast.85, bf16[4,3,128,128]{3,2,1,0:T(8,128)(2,1)S(1)} %bitcast.87, bf16[4,3]{1,0:T(4,128)(2,1)S(1)} %bitcast.89), kind=kOutput, calls=%fused_computation.10 | convolution fusion | flops 51183616 | bytes 917528 | tf_op jit(solution)/shard_map/clqbi,qbij->clqj/dot_general | solution.py:51
  5.2 0.2 copy.54
  5.3 0.9 %reshape.188 = bf16[4,2,8192]{2,1,0:T(2,128)(2,1)} reshape(bf16[512,2,64]{2,1,0:T(2,128)(2,1)S(1)} %bitcast.79) | data formatting | bytes 262144
  6.2 5.4 %all-to-all-start = ((bf16[4,2,8192]{2,1,0:T(2,128)(2,1)}), bf16[4,2,8192]{2,1,0:T(2,128)(2,1)S(1)}, u32[]{:S(2)}, u32[]{:S(2)}) async-start(bf16[4,2,8192]{2,1,0:T(2,128)(2,1)} %reshape.188), calls=%async_computation | async-start | bytes 262144 | tf_op jit(solution)/shard_map/all_to_all | solution.py:62
  11.6 0.0 copy-start.5
  11.7 0.7 %copy-done.5 = s32[1,2,3]{2,1,0:T(2,128)S(1)} copy-done((s32[1,2,3]{2,1,0:T(2,128)S(1)}, s32[1,2,3]{2,1,0:T(2,128)}, u32[]{:S(2)}) %copy-start.5) | copy-done | bytes 48
  12.3 0.1 reshape.134
  12.4 0.0 copy-start.6
  12.4 0.7 %copy-done.6 = s32[1,2,3]{2,1,0:T(2,128)S(1)} copy-done((s32[1,2,3]{2,1,0:T(2,128)S(1)}, s32[1,2,3]{2,1,0:T(2,128)}, u32[]{:S(2)}) %copy-start.6) | copy-done | bytes 48
  13.1 0.0 copy-start.1
  13.1 0.7 %copy-done.1 = s32[1,2,3]{2,1,0:T(2,128)S(1)} copy-done((s32[1,2,3]{2,1,0:T(2,128)S(1)}, s32[1,2,3]{2,1,0:T(2,128)}, u32[]{:S(2)}) %copy-start.1) | copy-done | bytes 48
  13.8 0.6 %gather_fusion.4 = s32[2,3]{1,0:T(2,128)S(1)} fusion(s32[2,3]{1,0:T(2,128)S(1)} %bitcast.88, s32[1024]{0:T(1024)S(1)} %pad_clamp_fusion.3), kind=kCustom, calls=%fused_computation.4 | custom fusion | bytes 56 | tf_op jit(solution)/shard_map/gather | solution.py:65
  14.3 1.6 %gather_fusion = bf16[6,128,128]{2,1,0:T(8,128)(2,1)S(1)} fusion(bf16[16,128,128]{2,1,0:T(8,128)(2,1)} %param.14, s32[1024]{0:T(1024)S(1)} %pad_clamp_fusion.4), kind=kCustom, calls=%fused_computation | custom fusion | bytes 393240 | tf_op jit(solution)/shard_map/gather | solution.py:58
  16.0 0.1 broadcast_multiply_fusion
  16.1 0.1 reshape.174
  16.1 0.6 %gather_fusion.1 = bf16[2,3,128,128]{3,2,1,0:T(8,128)(2,1)S(1)} fusion(bf16[2,3,128,128]{3,2,1,0:T(8,128)(2,1)S(1)} %broadcast_multiply_fusion, s32[1024]{0:T(1024)S(1)} %pad_clamp_fusion.3), kind=kCustom, calls=%fused_computation.1 | custom fusion | bytes 393224 | tf_op jit(solution)/shard_map/gather | solution.py:67
  16.8 0.0 all-to-all-done
  16.8 0.2 reshape.189
  17.0 0.2 copy.55
  17.2 0.6 %gather_fusion.5 = bf16[6,2,128,128]{3,2,1,0:T(8,128)(2,1)S(1)} fusion(bf16[2,2,128,128]{3,2,1,0:T(8,128)(2,1)S(1)} %bitcast.77, s32[1024]{0:T(1024)S(1)} %pad_clamp_fusion), kind=kCustom, calls=%fused_computation.5 | custom fusion | bytes 786456 | tf_op jit(solution)/shard_map/gather | solution.py:65
  17.8 0.2 fusion.3
  18.1 4.9 %collective-permute-start = (bf16[2,64,128]{2,1,0:T(8,128)(2,1)S(1)}, bf16[2,64,128]{2,1,0:T(8,128)(2,1)S(1)}, u32[]{:S(2)}, u32[]{:S(2)}) collective-permute-start(bf16[2,64,128]{2,1,0:T(8,128)(2,1)S(1)} %get-tuple-element.7), channel_id=1, source_target_pairs={{0,4},{4,8},{8,12},{1,5},{5,9},{9,13},{2,6},{6,10},{10,14},{3,7},{... | collective-permute-start | bytes 98312 | tf_op jit(solution)/shard_map/ppermute | solution.py:13
  23.0 1.9 %collective-permute-start.1 = (bf16[2,64,128]{2,1,0:T(8,128)(2,1)S(1)}, bf16[2,64,128]{2,1,0:T(8,128)(2,1)S(1)}, u32[]{:S(2)}, u32[]{:S(2)}) collective-permute-start(bf16[2,64,128]{2,1,0:T(8,128)(2,1)S(1)} %get-tuple-element.8), channel_id=1, source_target_pairs={{4,0},{8,4},{12,8},{5,1},{9,5},{13,9},{6,2},{10,6},{14,10},{7,3},{... | collective-permute-start | bytes 98312 | tf_op jit(solution)/shard_map/ppermute | solution.py:13
  25.0 0.0 collective-permute-done
  25.0 3.3 %collective-permute-done.1 = bf16[2,64,128]{2,1,0:T(8,128)(2,1)S(1)} collective-permute-done((bf16[2,64,128]{2,1,0:T(8,128)(2,1)S(1)}, bf16[2,64,128]{2,1,0:T(8,128)(2,1)S(1)}, u32[]{:S(2)}, u32[]{:S(2)}) %collective-permute-start.1) | collective-permute-done | bytes 32800 | tf_op jit(solution)/shard_map/ppermute | solution.py:13
  28.2 0.1 fusion.8
  28.3 0.7 %maximum_bitcast_fusion = bf16[1,2,256,128]{3,2,1,0:T(8,128)(2,1)} fusion(bf16[2,64,128]{2,1,0:T(8,128)(2,1)S(1)} %get-tuple-element.6, bf16[2,128,128]{2,1,0:T(8,128)(2,1)S(1)} %slice.26, bf16[2,64,128]{2,1,0:T(8,128)(2,1)S(1)} %get-tuple-element.5), kind=kLoop, calls=%fused_computation.16 | loop fusion | flops 393216 | bytes 262144 | tf_op jit(solution)/shard_map/broadcast_in_dim | solution.py:72
  (18 shorter events, 0.1 us)
Async XLA Ops:
  0.0 4.2 %copy-start = (bf16[16,128,128]{2,1,0:T(8,128)(2,1)S(1)}, bf16[16,128,128]{2,1,0:T(8,128)(2,1)}, u32[]{:S(2)}) copy-start(bf16[16,128,128]{2,1,0:T(8,128)(2,1)} %param.10) | copy-start | bytes 1572868
  1.0 0.7 %copy-start.2 = (s32[1,4,3]{1,0,2:T(1,128)S(1)}, s32[1,4,3]{1,0,2:T(1,128)}, u32[]{:S(2)}) copy-start(s32[1,4,3]{1,0,2:T(1,128)} %param.11) | copy-start | bytes 148
  1.9 0.7 %copy-start.3 = (s32[1,4,3]{1,0,2:T(1,128)S(1)}, s32[1,4,3]{1,0,2:T(1,128)}, u32[]{:S(2)}) copy-start(s32[1,4,3]{1,0,2:T(1,128)} %param.12) | copy-start | bytes 148
  2.7 0.7 %copy-start.4 = (s32[1,4,3]{1,0,2:T(1,128)S(1)}, s32[1,4,3]{1,0,2:T(1,128)}, u32[]{:S(2)}) copy-start(s32[1,4,3]{1,0,2:T(1,128)} %param.13) | copy-start | bytes 148
  6.2 10.5 %all-to-all-start = ((bf16[4,2,8192]{2,1,0:T(2,128)(2,1)}), bf16[4,2,8192]{2,1,0:T(2,128)(2,1)S(1)}, u32[]{:S(2)}, u32[]{:S(2)}) async-start(bf16[4,2,8192]{2,1,0:T(2,128)(2,1)} %reshape.188), calls=%async_computation | async-start | bytes 262144 | tf_op jit(solution)/shard_map/all_to_all | solution.py:62
  11.6 0.7 %copy-start.5 = (s32[1,2,3]{2,1,0:T(2,128)S(1)}, s32[1,2,3]{2,1,0:T(2,128)}, u32[]{:S(2)}) copy-start(s32[1,2,3]{2,1,0:T(2,128)} %param.16) | copy-start | bytes 76
  12.4 0.7 %copy-start.6 = (s32[1,2,3]{2,1,0:T(2,128)S(1)}, s32[1,2,3]{2,1,0:T(2,128)}, u32[]{:S(2)}) copy-start(s32[1,2,3]{2,1,0:T(2,128)} %param.17) | copy-start | bytes 76
  13.1 0.7 %copy-start.1 = (s32[1,2,3]{2,1,0:T(2,128)S(1)}, s32[1,2,3]{2,1,0:T(2,128)}, u32[]{:S(2)}) copy-start(s32[1,2,3]{2,1,0:T(2,128)} %param.15) | copy-start | bytes 76
  18.1 6.9 %collective-permute-start = (bf16[2,64,128]{2,1,0:T(8,128)(2,1)S(1)}, bf16[2,64,128]{2,1,0:T(8,128)(2,1)S(1)}, u32[]{:S(2)}, u32[]{:S(2)}) collective-permute-start(bf16[2,64,128]{2,1,0:T(8,128)(2,1)S(1)} %get-tuple-element.7), channel_id=1, source_target_pairs={{0,4},{4,8},{8,12},{1,5},{5,9},{9,13},{2,6},{6,10},{10,14},{3,7},{... | collective-permute-start | bytes 98312 | tf_op jit(solution)/shard_map/ppermute | solution.py:13
  23.0 5.2 %collective-permute-start.1 = (bf16[2,64,128]{2,1,0:T(8,128)(2,1)S(1)}, bf16[2,64,128]{2,1,0:T(8,128)(2,1)S(1)}, u32[]{:S(2)}, u32[]{:S(2)}) collective-permute-start(bf16[2,64,128]{2,1,0:T(8,128)(2,1)S(1)} %get-tuple-element.8), channel_id=1, source_target_pairs={{4,0},{8,4},{12,8},{5,1},{9,5},{13,9},{6,2},{10,6},{14,10},{7,3},{... | collective-permute-start | bytes 98312 | tf_op jit(solution)/shard_map/ppermute | solution.py:13
where the time goes:
time: 29.4 us; the launch traced here: 29 us
  starting transfers between devices  12.2 us (41%)
  local copies, waits for them, and re-layouts  11.8 us (40%)
  waiting for transfers between devices  3.26 us (11%)
  other arithmetic  0.91 us (3%)
  matrix products  0.57 us (2%)
    ppermute x2, starting transfers between devices, passed_along(): return lax.ppermute(block, axis, route)  6.83 us
    all_to_all x1, starting transfers between devices, on_device(): lax.all_to_all(along_samples, 'tile', split_axis=2, concat_axis=1, tiled=...  5.41 us
    unnamed x16, local copies, waits for them, and re-layouts  5.14 us
    ppermute x2, waiting for transfers between devices, passed_along(): return lax.ppermute(block, axis, route)  3.26 us
    gather x1, local copies, waits for them, and re-layouts, on_device(): column_bank[column_pick[0]]  1.62 us
    gather x2, local copies, waits for them, and re-layouts, on_device(): picked = line_tiles[:, band_table[every_id]]  1.18 us
    another operation x2, local copies, waits for them, and re-layouts, on_device(): blocks = image.reshape(channels, lin_dev, column_blocks, BLOCK)  1.02 us
    broadcast_in_dim x1, other arithmetic, on_device(): return gridded[None]  0.67 us
  transfers between devices with their start and end apart: 3, of which 1 were waited for; matrix products, arithmetic and copies ran while one was open for 11% of the time, Pallas kernels for 0%

commit v1 on v0

--- a/solution.py
+++ b/solution.py
@@ -59,7 +59,15 @@
     )
     band_table = column_index[0]
     every_id = jnp.arange(line_blocks, dtype=jnp.int32)
-    moved = lax.all_to_all(along_samples, "tile", split_axis=2, concat_axis=1, tiled=True)
+    ways, here = (lax.axis_size("tile"), lax.axis_index("tile"))
+    width = along_samples.shape[2] // ways
+    turned = jnp.roll(along_samples, -here * width, axis=2)
+    got = [lax.slice_in_dim(turned, 0, width, axis=2)]
+    for far in range(1, ways):
+        sent = lax.slice_in_dim(turned, far * width, (far + 1) * width, axis=2)
+        got.append(lax.ppermute(sent, "tile", [(d, (d + far) % ways) for d in range(ways)]))
+    line = jnp.concatenate(got[::-1], axis=1)
+    moved = jnp.roll(line, (here + 1) * got[0].shape[1], axis=1)
     count = moved.shape[0]
     line_tiles = moved.reshape(count, line_blocks, BLOCK, BLOCK)
     picked = line_tiles[:, band_table[every_id]]

time: 29.4 us -> 26.4 us (0.90)
  local copies, waits for them, and re-layouts: 11.8 us -> 9.86 us
  starting transfers between devices: 12.2 us -> 11.1 us
    all_to_all x1 -> x0, starting transfers between devices: 5.41 us -> none  [on_device(): lax.all_to_all(along_samples, 'tile', split_axis=2, concat_axis=1, tiled=...]
    ppermute x0 -> x3, starting transfers between devices: none -> 4.65 us  [on_device(): lax.ppermute(sent, 'tile', [(d, (d + far) % ways) for d in range(ways)])]
    unnamed x16 -> x21, local copies, waits for them, and re-layouts: 5.14 us -> 3.53 us
    ppermute x2, starting transfers between devices: 6.83 us -> 6.49 us  [passed_along(): return lax.ppermute(block, axis, route)]
  transfers between devices with their start and end apart: 3 -> 5, of which waited for: 1 -> 1; matrix products, arithmetic and copies ran while one was open for 11% -> 12% of each run, Pallas kernels for 0% -> 0%
where the time goes in v1:
time: 26.4 us; the launch traced here: 26.1 us
  starting transfers between devices  11.1 us (42%)
  local copies, waits for them, and re-layouts  9.86 us (37%)
  waiting for transfers between devices  3.27 us (12%)
  other arithmetic  0.97 us (4%)
  matrix products  0.57 us (2%)
  between operations  0.31 us (1%)
    ppermute x2, starting transfers between devices, passed_along(): return lax.ppermute(block, axis, route)  6.49 us
    ppermute x3, starting transfers between devices, on_device(): lax.ppermute(sent, 'tile', [(d, (d + far) % ways) for d in range(ways)])  4.65 us
    unnamed x21, local copies, waits for them, and re-layouts  3.53 us
    ppermute x2, waiting for transfers between devices, passed_along(): return lax.ppermute(block, axis, route)  3.26 us
    gather x1, local copies, waits for them, and re-layouts, on_device(): column_bank[column_pick[0]]  1.62 us
    gather x2, local copies, waits for them, and re-layouts, on_device(): picked = line_tiles[:, band_table[every_id]]  1.18 us
    another operation x2, local copies, waits for them, and re-layouts, on_device(): blocks = image.reshape(channels, lin_dev, column_blocks, BLOCK)  0.96 us
    broadcast_in_dim x1, other arithmetic, on_device(): return gridded[None]  0.67 us
  transfers between devices with their start and end apart: 5, of which 1 were waited for; matrix products, arithmetic and copies ran while one was open for 12% of the time, Pallas kernels for 0%

profile of v1, /device:TPU:1, one launch (start us, length us, event | category | flops | bytes accessed | tf_op | source)
XLA Modules:
  0.0 26.1 jit_solution(454668579128610420)
XLA Ops:
  0.0 0.0 copy-start
  0.0 0.0 copy-start.2
  0.0 0.7 %copy-done.2 = s32[1,4,3]{1,0,2:T(1,128)S(1)} copy-done((s32[1,4,3]{1,0,2:T(1,128)S(1)}, s32[1,4,3]{1,0,2:T(1,128)}, u32[]{:S(2)}) %copy-start.2) | copy-done | bytes 72
  0.7 0.1 copy.20
  0.8 0.0 copy-start.3
  0.8 0.1 reshape.149
  0.9 0.6 %copy-done.3 = s32[1,4,3]{1,0,2:T(1,128)S(1)} copy-done((s32[1,4,3]{1,0,2:T(1,128)S(1)}, s32[1,4,3]{1,0,2:T(1,128)}, u32[]{:S(2)}) %copy-start.3) | copy-done | bytes 72
  1.5 0.1 copy.22
  1.6 0.1 reshape.157
  1.7 0.9 %reshape_squeeze.3 = bf16[2,64,4,128]{3,2,1,0:T(4,128)(2,1)S(1)} reshape(bf16[1,2,64,512]{3,2,1,0:T(8,128)(2,1)} %param.9) | data formatting | bytes 262144 | tf_op jit(solution)/shard_map/reshape;squeeze | solution.py:48
  2.7 0.0 copy-start.4
  2.7 0.6 %copy-done.4 = s32[1,4,3]{1,0,2:T(1,128)S(1)} copy-done((s32[1,4,3]{1,0,2:T(1,128)S(1)}, s32[1,4,3]{1,0,2:T(1,128)}, u32[]{:S(2)}) %copy-start.4) | copy-done | bytes 72
  3.3 0.1 copy.21
  3.5 0.6 %gather_fusion.3 = bf16[12,2,64,128]{3,2,1,0:T(8,128)(2,1)S(1)} fusion(bf16[2,64,4,128]{3,1,2,0:T(8,128)(2,1)S(1)} %copy.23, s32[1024]{0:T(1024)S(1)} %get-tuple-element.14), kind=kCustom, calls=%fused_computation.3 | custom fusion | bytes 786480 | tf_op jit(solution)/shard_map/gather | solution.py:49
  4.1 0.0 copy-done
  4.1 0.6 %gather_fusion.2 = bf16[12,128,128]{2,1,0:T(8,128)(2,1)S(1)} fusion(bf16[16,128,128]{2,1,0:T(8,128)(2,1)S(1)} %copy-done, s32[1024]{0:T(1024)S(1)} %get-tuple-element.15), kind=kCustom, calls=%fused_computation.2 | custom fusion | bytes 786480 | tf_op jit(solution)/shard_map/gather | solution.py:50
  4.7 0.3 %fusion.2 = bf16[4,2,8,8,128]{4,3,2,1,0:T(8,128)(2,1)S(1)} fusion(bf16[2,64,4,3,128]{4,1,0,3,2:T(8,128)(2,1)S(1)} %bitcast.82, bf16[4,3,128,128]{3,2,1,0:T(8,128)(2,1)S(1)} %bitcast.84, bf16[4,3]{1,0:T(4,128)(2,1)S(1)} %bitcast.86), kind=kOutput, calls=%fused_computation.10 | convolution fusion | flops 51183616 | bytes 917528 | tf_op jit(solution)/shard_map/clqbi,qbij->clqj/dot_general | solution.py:51
  5.1 0.1 fusion.8
  5.2 4.2 %collective-permute-start = (bf16[2,64,128]{2,1,0:T(8,128)(2,1)S(1)}, bf16[2,64,128]{2,1,0:T(8,128)(2,1)S(1)}, u32[]{:S(2)}, u32[]{:S(2)}) collective-permute-start(bf16[2,64,128]{2,1,0:T(8,128)(2,1)S(1)} %get-tuple-element.11), channel_id=1, source_target_pairs={{0,3},{1,0},{2,1},{3,2},{4,7},{5,4},{6,5},{7,6},{8,11},{9,8},{10,9... | collective-permute-start | bytes 98312 | tf_op jit(solution)/shard_map/ppermute | solution.py:68
  9.4 0.0 collective-permute-start.1
  9.4 0.5 %collective-permute-start.2 = (bf16[2,64,128]{2,1,0:T(8,128)(2,1)S(1)}, bf16[2,64,128]{2,1,0:T(8,128)(2,1)S(1)}, u32[]{:S(2)}, u32[]{:S(2)}) collective-permute-start(bf16[2,64,128]{2,1,0:T(8,128)(2,1)S(1)} %get-tuple-element.9), channel_id=1, source_target_pairs={{0,1},{1,2},{2,3},{3,0},{4,5},{5,6},{6,7},{7,4},{8,9},{9,10},{10,1... | collective-permute-start | bytes 98312 | tf_op jit(solution)/shard_map/ppermute | solution.py:68
  9.9 0.0 copy-start.1
  9.9 0.7 %copy-done.1 = s32[1,2,3]{2,1,0:T(2,128)S(1)} copy-done((s32[1,2,3]{2,1,0:T(2,128)S(1)}, s32[1,2,3]{2,1,0:T(2,128)}, u32[]{:S(2)}) %copy-start.1) | copy-done | bytes 48
  10.5 0.0 copy-start.5
  10.5 0.6 %gather_fusion.4 = s32[2,3]{1,0:T(2,128)S(1)} fusion(s32[2,3]{1,0:T(2,128)S(1)} %bitcast.85, s32[1024]{0:T(1024)S(1)} %pad_clamp_fusion.3), kind=kCustom, calls=%fused_computation.4 | custom fusion | bytes 56 | tf_op jit(solution)/shard_map/gather | solution.py:73
  11.1 0.1 copy-done.5
  11.2 0.1 reshape.173
  11.3 0.1 reshape.133
  11.4 0.0 copy-start.6
  11.4 0.7 %copy-done.6 = s32[1,2,3]{2,1,0:T(2,128)S(1)} copy-done((s32[1,2,3]{2,1,0:T(2,128)S(1)}, s32[1,2,3]{2,1,0:T(2,128)}, u32[]{:S(2)}) %copy-start.6) | copy-done | bytes 48
  12.1 1.6 %gather_fusion = bf16[6,128,128]{2,1,0:T(8,128)(2,1)S(1)} fusion(bf16[16,128,128]{2,1,0:T(8,128)(2,1)} %param.14, s32[1024]{0:T(1024)S(1)} %pad_clamp_fusion.4), kind=kCustom, calls=%fused_computation | custom fusion | bytes 393240 | tf_op jit(solution)/shard_map/gather | solution.py:58
  13.7 0.1 broadcast_multiply_fusion
  13.8 0.6 %gather_fusion.1 = bf16[2,3,128,128]{3,2,1,0:T(8,128)(2,1)S(1)} fusion(bf16[2,3,128,128]{3,2,1,0:T(8,128)(2,1)S(1)} %broadcast_multiply_fusion, s32[1024]{0:T(1024)S(1)} %pad_clamp_fusion.3), kind=kCustom, calls=%fused_computation.1 | custom fusion | bytes 393224 | tf_op jit(solution)/shard_map/gather | solution.py:75
  14.4 0.0 collective-permute-done
  14.5 0.0 collective-permute-done.1
  14.5 0.0 collective-permute-done.2
  14.6 0.6 %gather_fusion.5 = bf16[6,2,128,128]{3,2,1,0:T(8,128)(2,1)S(1)} fusion(bf16[2,2,128,128]{3,2,1,0:T(8,128)(2,1)S(1)} %bitcast.76, s32[1024]{0:T(1024)S(1)} %pad_clamp_fusion), kind=kCustom, calls=%fused_computation.5 | custom fusion | bytes 786456 | tf_op jit(solution)/shard_map/gather | solution.py:73
  15.2 0.2 fusion.3
  15.5 4.6 %collective-permute-start.3 = (bf16[2,64,128]{2,1,0:T(8,128)(2,1)S(1)}, bf16[2,64,128]{2,1,0:T(8,128)(2,1)S(1)}, u32[]{:S(2)}, u32[]{:S(2)}) collective-permute-start(bf16[2,64,128]{2,1,0:T(8,128)(2,1)S(1)} %get-tuple-element.7), channel_id=1, source_target_pairs={{0,4},{4,8},{8,12},{1,5},{5,9},{9,13},{2,6},{6,10},{10,14},{3,7},{... | collective-permute-start | bytes 98312 | tf_op jit(solution)/shard_map/ppermute | solution.py:13
  20.1 1.9 %collective-permute-start.4 = (bf16[2,64,128]{2,1,0:T(8,128)(2,1)S(1)}, bf16[2,64,128]{2,1,0:T(8,128)(2,1)S(1)}, u32[]{:S(2)}, u32[]{:S(2)}) collective-permute-start(bf16[2,64,128]{2,1,0:T(8,128)(2,1)S(1)} %get-tuple-element.8), channel_id=1, source_target_pairs={{4,0},{8,4},{12,8},{5,1},{9,5},{13,9},{6,2},{10,6},{14,10},{7,3},{... | collective-permute-start | bytes 98312 | tf_op jit(solution)/shard_map/ppermute | solution.py:13
  22.1 0.0 collective-permute-done.3
  22.1 3.3 %collective-permute-done.4 = bf16[2,64,128]{2,1,0:T(8,128)(2,1)S(1)} collective-permute-done((bf16[2,64,128]{2,1,0:T(8,128)(2,1)S(1)}, bf16[2,64,128]{2,1,0:T(8,128)(2,1)S(1)}, u32[]{:S(2)}, u32[]{:S(2)}) %collective-permute-start.4) | collective-permute-done | bytes 32800 | tf_op jit(solution)/shard_map/ppermute | solution.py:13
  25.3 0.1 fusion.9
  25.4 0.7 %maximum_bitcast_fusion = bf16[1,2,256,128]{3,2,1,0:T(8,128)(2,1)} fusion(bf16[2,64,128]{2,1,0:T(8,128)(2,1)S(1)} %get-tuple-element.6, bf16[2,128,128]{2,1,0:T(8,128)(2,1)S(1)} %slice.46, bf16[2,64,128]{2,1,0:T(8,128)(2,1)S(1)} %get-tuple-element.5), kind=kLoop, calls=%fused_computation.20 | loop fusion | flops 393216 | bytes 262144 | tf_op jit(solution)/shard_map/broadcast_in_dim | solution.py:80
  (26 shorter events, 0.3 us)
Async XLA Ops:
  0.0 4.1 %copy-start = (bf16[16,128,128]{2,1,0:T(8,128)(2,1)S(1)}, bf16[16,128,128]{2,1,0:T(8,128)(2,1)}, u32[]{:S(2)}) copy-start(bf16[16,128,128]{2,1,0:T(8,128)(2,1)} %param.10) | copy-start | bytes 1572868
  0.0 0.7 %copy-start.2 = (s32[1,4,3]{1,0,2:T(1,128)S(1)}, s32[1,4,3]{1,0,2:T(1,128)}, u32[]{:S(2)}) copy-start(s32[1,4,3]{1,0,2:T(1,128)} %param.12) | copy-start | bytes 148
  0.8 0.7 %copy-start.3 = (s32[1,4,3]{1,0,2:T(1,128)S(1)}, s32[1,4,3]{1,0,2:T(1,128)}, u32[]{:S(2)}) copy-start(s32[1,4,3]{1,0,2:T(1,128)} %param.11) | copy-start | bytes 148
  2.7 0.7 %copy-start.4 = (s32[1,4,3]{1,0,2:T(1,128)S(1)}, s32[1,4,3]{1,0,2:T(1,128)}, u32[]{:S(2)}) copy-start(s32[1,4,3]{1,0,2:T(1,128)} %param.13) | copy-start | bytes 148
  5.2 9.2 %collective-permute-start = (bf16[2,64,128]{2,1,0:T(8,128)(2,1)S(1)}, bf16[2,64,128]{2,1,0:T(8,128)(2,1)S(1)}, u32[]{:S(2)}, u32[]{:S(2)}) collective-permute-start(bf16[2,64,128]{2,1,0:T(8,128)(2,1)S(1)} %get-tuple-element.11), channel_id=1, source_target_pairs={{0,3},{1,0},{2,1},{3,2},{4,7},{5,4},{6,5},{7,6},{8,11},{9,8},{10,9... | collective-permute-start | bytes 98312 | tf_op jit(solution)/shard_map/ppermute | solution.py:68
  9.4 5.1 %collective-permute-start.1 = (bf16[2,64,128]{2,1,0:T(8,128)(2,1)S(1)}, bf16[2,64,128]{2,1,0:T(8,128)(2,1)S(1)}, u32[]{:S(2)}, u32[]{:S(2)}) collective-permute-start(bf16[2,64,128]{2,1,0:T(8,128)(2,1)S(1)} %get-tuple-element.10), channel_id=1, source_target_pairs={{0,2},{1,3},{2,0},{3,1},{4,6},{5,7},{6,4},{7,5},{8,10},{9,11},{10,... | collective-permute-start | bytes 98312 | tf_op jit(solution)/shard_map/ppermute | solution.py:68
  9.4 5.1 %collective-permute-start.2 = (bf16[2,64,128]{2,1,0:T(8,128)(2,1)S(1)}, bf16[2,64,128]{2,1,0:T(8,128)(2,1)S(1)}, u32[]{:S(2)}, u32[]{:S(2)}) collective-permute-start(bf16[2,64,128]{2,1,0:T(8,128)(2,1)S(1)} %get-tuple-element.9), channel_id=1, source_target_pairs={{0,1},{1,2},{2,3},{3,0},{4,5},{5,6},{6,7},{7,4},{8,9},{9,10},{10,1... | collective-permute-start | bytes 98312 | tf_op jit(solution)/shard_map/ppermute | solution.py:68
  9.9 0.7 %copy-start.1 = (s32[1,2,3]{2,1,0:T(2,128)S(1)}, s32[1,2,3]{2,1,0:T(2,128)}, u32[]{:S(2)}) copy-start(s32[1,2,3]{2,1,0:T(2,128)} %param.15) | copy-start | bytes 76
  10.5 0.7 %copy-start.5 = (s32[1,2,3]{2,1,0:T(2,128)S(1)}, s32[1,2,3]{2,1,0:T(2,128)}, u32[]{:S(2)}) copy-start(s32[1,2,3]{2,1,0:T(2,128)} %param.16) | copy-start | bytes 76
  11.4 0.7 %copy-start.6 = (s32[1,2,3]{2,1,0:T(2,128)S(1)}, s32[1,2,3]{2,1,0:T(2,128)}, u32[]{:S(2)}) copy-start(s32[1,2,3]{2,1,0:T(2,128)} %param.17) | copy-start | bytes 76
  15.5 6.5 %collective-permute-start.3 = (bf16[2,64,128]{2,1,0:T(8,128)(2,1)S(1)}, bf16[2,64,128]{2,1,0:T(8,128)(2,1)S(1)}, u32[]{:S(2)}, u32[]{:S(2)}) collective-permute-start(bf16[2,64,128]{2,1,0:T(8,128)(2,1)S(1)} %get-tuple-element.7), channel_id=1, source_target_pairs={{0,4},{4,8},{8,12},{1,5},{5,9},{9,13},{2,6},{6,10},{10,14},{3,7},{... | collective-permute-start | bytes 98312 | tf_op jit(solution)/shard_map/ppermute | solution.py:13
  20.1 5.2 %collective-permute-start.4 = (bf16[2,64,128]{2,1,0:T(8,128)(2,1)S(1)}, bf16[2,64,128]{2,1,0:T(8,128)(2,1)S(1)}, u32[]{:S(2)}, u32[]{:S(2)}) collective-permute-start(bf16[2,64,128]{2,1,0:T(8,128)(2,1)S(1)} %get-tuple-element.8), channel_id=1, source_target_pairs={{4,0},{8,4},{12,8},{5,1},{9,5},{13,9},{6,2},{10,6},{14,10},{7,3},{... | collective-permute-start | bytes 98312 | tf_op jit(solution)/shard_map/ppermute | solution.py:13
